TPU v7x, 32 devices: a whole 2x2x4 slice. The times are simulated.
32 devices in a mesh: dp: 8 (over z, y), mp: 4 (over x, core).
Axes of the slice: x: 2, y: 2, z: 4, core: 2. Of those that a mesh axis runs over, the one named last changes fastest.
Arguments:
- residual: bfloat16 [16384, 768], P('dp', 'mp'), may hold values from -6 to 6, as said below
- lengths: int32 [8, 4], P('dp'), may hold values from 0 to 2048, as said below
- gain_one: float32 [768], P('mp'), may hold values from 0.5 to 1.5
- input_weight: bfloat16 [3, 768, 768], P(None, None, 'mp'), may hold values from -0.21875 to 0.21875
- input_bias: float32 [2, 768], P(None, 'mp'), may hold values from -1.8 to 1.8
- output_weight: bfloat16 [768, 768], P('mp'), may hold values from -2.5 to 2.5
- output_bias: float32 [768], P('mp'), may hold values from -1.8 to 1.8
- gain_two: float32 [768], P('mp'), may hold values from 0.5 to 1.5
- expand_weight: bfloat16 [768, 3072], P(None, 'mp'), may hold values from -0.21875 to 0.21875
- expand_bias: float32 [3072], P('mp'), may hold values from -1.8 to 1.8
- reduce_weight: bfloat16 [3072, 768], P('mp'), may hold values from -0.109375 to 0.109375
- reduce_bias: float32 [768], P('mp'), may hold values from -1.8 to 1.8
- cotangent: bfloat16 [16384, 768], P('dp', 'mp'), may hold values from -6 to 6
Outputs:
- residual_out: bfloat16 [16384, 768], P('dp', 'mp')
- residual_grad: bfloat16 [16384, 768], P('dp', 'mp')
- input_weight_grad: float32 [3, 768, 768], P(None, None, 'mp')
- input_bias_grad: float32 [2, 768], P(None, 'mp')
- output_weight_grad: float32 [768, 768], P('mp')
- output_bias_grad: float32 [768], P('mp')
- gain_one_grad: float32 [768], P('mp')
- gain_two_grad: float32 [768], P('mp')
- expand_weight_grad: float32 [768, 3072], P(None, 'mp')
- expand_bias_grad: float32 [3072], P('mp')
- reduce_weight_grad: float32 [3072, 768], P('mp')
- reduce_bias_grad: float32 [768], P('mp')
- residual_rms: float32 [], replicated
- live_count: int32 [], replicated
Inputs may be any that keep to these rules, and one draw needn't show every extreme that they name: Each row holds one group's sequence lengths by slot: first some of 2048, then some of 512, then zeros for unused slots; a row sums to at most 2048, and the first row holds a sequence of 2048. `residual`: column 767 is not read.
All inputs are finite; a program needn't handle non-finite values.
Results may differ from a plain program's by a relative error of at most 0.015.
Values may be sent and summed in bfloat16 or wider, within the bound.
A program may use at most 128 MiB of HBM per device.

v0:
```python
import jax
import jax.numpy as jnp
from jax import lax
from jax.sharding import PartitionSpec as P

D = 768
HEAD = 64
SHORT = 512
LONG = 2048
EPSILON = 1e-05
SCORE_SCALE = 0.125
NEGATIVE = -1e30


def smooth(inputs):
    return jax.nn.gelu(inputs, approximate=True)


def layout(width):
    columns = lax.axis_index("mp") * width + jnp.arange(width)
    return (columns < D - 1, columns == D - 1)


def segments(seq_lengths, row_count):
    seq_ends = jnp.cumsum(seq_lengths)
    positions = jnp.arange(row_count)
    segment = jnp.sum((positions[:, None] >= seq_ends[None, :]).astype(jnp.int32), axis=1)
    return (segment, positions < seq_ends[-1])


def window(row_start, row_count, segment, live_rows):
    key_start = jnp.clip(row_start + SHORT - LONG, 0, row_count - LONG)
    query_pos = row_start + jnp.arange(SHORT)
    key_pos = key_start + jnp.arange(LONG)
    query_seg = lax.dynamic_slice_in_dim(segment, row_start, SHORT)
    query_live = lax.dynamic_slice_in_dim(live_rows, row_start, SHORT)
    causal = key_pos[None, :] <= query_pos[:, None]
    allowed = (query_seg[:, None] == segment[None, :]) & causal & query_live[:, None]
    return (key_start, allowed | (key_pos[None, :] == query_pos[:, None]))


def column_sums(values):
    return lax.psum((jnp.sum(values, axis=1), jnp.sum(values * values, axis=1)), "mp")


def gather_normed(normed):
    return lax.all_gather(normed, "mp", axis=1, tiled=True)


def sum_branch(partial_rows, bias_vec):
    return (
        lax.psum_scatter(partial_rows, "mp", scatter_dimension=1, tiled=True) + bias_vec[None, :],
        None,
    )


def spread_grads(grad_rows):
    return lax.all_gather(grad_rows, "mp", axis=1, tiled=True)


def feature_sums(partial_rows):
    return lax.psum_scatter(
        partial_rows.astype(jnp.bfloat16), "mp", scatter_dimension=1, tiled=True
    ).astype(jnp.float32)


def normalize(values, row_total, row_squares, pad_mask, gain_vec):
    decompressed = jnp.where(pad_mask[None, :], -row_total[:, None], values)
    inverse = lax.rsqrt((row_squares + row_total * row_total) / D + EPSILON)
    return (decompressed, inverse, decompressed * inverse[:, None] * gain_vec[None, :])


def add_branch(values, branch, stored):
    kept = stored[None, :]
    row_mean = lax.psum(jnp.sum(branch, axis=1), "mp") / D
    result = values + jnp.where(kept, branch - row_mean[:, None], 0.0)
    new_total, new_squares = column_sums(result)
    return (result, new_total, new_squares)


def attend_forward(queries, key_rows, value_rows, segment, live_rows):
    row_count = queries.shape[0]

    def attend_block(block_index):
        row_start = block_index * SHORT
        key_start, allowed = window(row_start, row_count, segment, live_rows)
        query_block = lax.dynamic_slice_in_dim(queries, row_start, SHORT, 0)
        scores = (
            jnp.einsum("qhd,khd->hqk", query_block, key_rows, preferred_element_type=jnp.float32)
            * SCORE_SCALE
        )
        scores = jnp.where(allowed[None], scores, NEGATIVE)
        row_max = jnp.max(scores, axis=2, keepdims=True)
        weights = jnp.exp(scores - row_max)
        row_sum = jnp.sum(weights, axis=2, keepdims=True)
        attn_probs = (weights / row_sum).astype(jnp.bfloat16)
        result = jnp.einsum(
            "hqk,khd->qhd", attn_probs, value_rows, preferred_element_type=jnp.float32
        )
        return (result.astype(jnp.bfloat16), (row_max + jnp.log(row_sum))[:, :, 0])

    blocks, log_totals = lax.map(attend_block, jnp.arange(row_count // SHORT, dtype=jnp.int32))
    return (blocks.reshape(row_count, queries.shape[1], queries.shape[2]), log_totals)


def attend_backward(queries, key_rows, value_rows, grad_mixed, log_totals, segment, live_rows):
    row_count = queries.shape[0]

    def step(block_index, running):
        grad_queries, grad_keys, grad_values = running
        row_start = block_index * SHORT
        key_start, allowed = window(row_start, row_count, segment, live_rows)
        query_block = lax.dynamic_slice_in_dim(queries, row_start, SHORT, 0)
        grad_block = lax.dynamic_slice_in_dim(grad_mixed, row_start, SHORT, 0)
        scores = (
            jnp.einsum("qhd,khd->hqk", query_block, key_rows, preferred_element_type=jnp.float32)
            * SCORE_SCALE
        )
        scores = jnp.where(allowed[None], scores, NEGATIVE)
        attn_probs = jnp.exp(scores - log_totals[block_index][:, :, None])
        grad_probs = jnp.einsum(
            "qhd,khd->hqk", grad_block, value_rows, preferred_element_type=jnp.float32
        )
        centered = grad_probs - jnp.sum(attn_probs * grad_probs, axis=2, keepdims=True)
        grad_scores = (attn_probs * centered).astype(jnp.bfloat16)
        query_part = (
            jnp.einsum("hqk,khd->qhd", grad_scores, key_rows, preferred_element_type=jnp.float32)
            * SCORE_SCALE
        )
        key_part = (
            jnp.einsum("hqk,qhd->khd", grad_scores, query_block, preferred_element_type=jnp.float32)
            * SCORE_SCALE
        )
        value_part = jnp.einsum(
            "hqk,qhd->khd",
            attn_probs.astype(jnp.bfloat16),
            grad_block,
            preferred_element_type=jnp.float32,
        )
        grad_queries = lax.dynamic_update_slice_in_dim(grad_queries, query_part, row_start, 0)
        grad_keys = grad_keys + key_part
        grad_values = grad_values + value_part
        return (grad_queries, grad_keys, grad_values)

    empty = jnp.zeros(queries.shape, jnp.float32)
    return lax.fori_loop(0, row_count // SHORT, step, (empty, empty, empty))


def on_device(
    residual,
    lengths,
    gain_one,
    input_weight,
    input_bias,
    output_weight,
    output_bias,
    gain_two,
    expand_weight,
    expand_bias,
    reduce_weight,
    reduce_bias,
    cotangent,
):
    row_count, width = residual.shape
    heads_here = width // HEAD
    stored, pad_mask = layout(width)
    segment, live_rows = segments(lengths[0], row_count)
    live_count = lax.psum(jnp.sum(lengths), "dp")
    values = jnp.where(stored[None, :], residual.astype(jnp.float32), 0.0)
    row_total, row_squares = column_sums(values)
    full_one, inverse_one, normed_one = normalize(
        values, row_total, row_squares, pad_mask, gain_one
    )
    rows_one = gather_normed(normed_one.astype(jnp.bfloat16))
    projected = jnp.einsum(
        "td,cde->cte", rows_one, input_weight, preferred_element_type=jnp.float32
    )
    queries = (
        (projected[0] + input_bias[0][None, :])
        .astype(jnp.bfloat16)
        .reshape(row_count, heads_here, HEAD)
    )
    key_rows = projected[1].astype(jnp.bfloat16).reshape(row_count, heads_here, HEAD)
    value_rows = (
        (projected[2] + input_bias[1][None, :])
        .astype(jnp.bfloat16)
        .reshape(row_count, heads_here, HEAD)
    )
    mixed, log_totals = attend_forward(queries, key_rows, value_rows, segment, live_rows)
    mixed = mixed.reshape(row_count, width)
    branch_one, branch_one_total = sum_branch(
        jnp.dot(mixed, output_weight, preferred_element_type=jnp.float32), output_bias
    )
    values_one, total_one, squares_one = add_branch(values, branch_one, stored)
    full_two, inverse_two, normed_two = normalize(
        values_one, total_one, squares_one, pad_mask, gain_two
    )
    rows_two = gather_normed(normed_two.astype(jnp.bfloat16))
    hidden = (
        jnp.dot(rows_two, expand_weight, preferred_element_type=jnp.float32) + expand_bias[None, :]
    )
    active = smooth(hidden).astype(jnp.bfloat16)
    branch_two, branch_two_total = sum_branch(
        jnp.dot(active, reduce_weight, preferred_element_type=jnp.float32), reduce_bias
    )
    values_two, total_two, squares_two = add_branch(values_one, branch_two, stored)
    residual_out = values_two.astype(jnp.bfloat16)
    square_part = jnp.sum(jnp.where(live_rows, squares_two + total_two * total_two, 0.0))
    gradients = jnp.where(stored[None, :], cotangent.astype(jnp.float32), 0.0)
    grad_total = lax.psum(jnp.sum(gradients, axis=1), "mp")
    grad_branch_two = gradients - grad_total[:, None] / D
    reduce_bias_grad = jnp.sum(grad_branch_two, axis=0)
    rows_grad_two = spread_grads(grad_branch_two.astype(jnp.bfloat16))
    reduce_weight_grad = jnp.einsum(
        "tf,td->fd", active, rows_grad_two, preferred_element_type=jnp.float32
    )
    grad_active = jnp.einsum(
        "td,fd->tf", rows_grad_two, reduce_weight, preferred_element_type=jnp.float32
    )
    grad_hidden = jax.vjp(smooth, hidden)[1](grad_active)[0].astype(jnp.bfloat16)
    expand_bias_grad = jnp.sum(grad_hidden, axis=0, dtype=jnp.float32)
    expand_weight_grad = jnp.einsum(
        "td,tf->df", rows_two, grad_hidden, preferred_element_type=jnp.float32
    )
    grad_normed_two = feature_sums(
        jnp.einsum("tf,df->td", grad_hidden, expand_weight, preferred_element_type=jnp.float32)
    )
    gain_two_grad = jnp.sum(grad_normed_two * full_two * inverse_two[:, None], axis=0)
    scaled_two = grad_normed_two * gain_two[None, :]
    projected_two, scaled_total, pad_term = lax.psum(
        (
            jnp.sum(scaled_two * full_two, axis=1),
            jnp.sum(scaled_two, axis=1),
            jnp.sum(jnp.where(pad_mask[None, :], scaled_two, 0.0), axis=1),
        ),
        "mp",
    )
    inverse_cube = inverse_two**3 / D
    grad_full = (
        inverse_two[:, None] * scaled_two - full_two * (inverse_cube * projected_two)[:, None]
    )
    grad_pad = inverse_two * pad_term + total_one * inverse_cube * projected_two
    grad_one = gradients + jnp.where(stored[None, :], grad_full - grad_pad[:, None], 0.0)
    stored_total = grad_total + inverse_two * scaled_total - D * grad_pad
    grad_branch_one = grad_one - stored_total[:, None] / D
    output_bias_grad = jnp.sum(grad_branch_one, axis=0)
    rows_grad_one = spread_grads(grad_branch_one.astype(jnp.bfloat16))
    output_weight_grad = jnp.einsum(
        "tc,td->cd", mixed, rows_grad_one, preferred_element_type=jnp.float32
    )
    grad_mixed = jnp.einsum(
        "td,cd->tc", rows_grad_one, output_weight, preferred_element_type=jnp.float32
    ).astype(jnp.bfloat16)
    query_grads, key_grads, value_grads = attend_backward(
        queries,
        key_rows,
        value_rows,
        grad_mixed.reshape(row_count, heads_here, HEAD),
        log_totals,
        segment,
        live_rows,
    )
    grad_inputs = (
        jnp.stack([query_grads, key_grads, value_grads])
        .astype(jnp.bfloat16)
        .reshape(3, row_count, width)
    )
    input_bias_grad = jnp.stack(
        [
            jnp.sum(grad_inputs[0], axis=0, dtype=jnp.float32),
            jnp.sum(grad_inputs[2], axis=0, dtype=jnp.float32),
        ]
    )
    input_weight_grad = jnp.einsum(
        "td,cte->cde", rows_one, grad_inputs, preferred_element_type=jnp.float32
    )
    grad_normed_one = feature_sums(
        jnp.einsum("cte,cde->td", grad_inputs, input_weight, preferred_element_type=jnp.float32)
    )
    gain_one_grad = jnp.sum(grad_normed_one * full_one * inverse_one[:, None], axis=0)
    scaled_one = grad_normed_one * gain_one[None, :]
    projected_one, pad_first = lax.psum(
        (
            jnp.sum(scaled_one * full_one, axis=1),
            jnp.sum(jnp.where(pad_mask[None, :], scaled_one, 0.0), axis=1),
        ),
        "mp",
    )
    inverse_first = inverse_one**3 / D
    grad_first = (
        inverse_one[:, None] * scaled_one - full_one * (inverse_first * projected_one)[:, None]
    )
    grad_pad_first = inverse_one * pad_first + row_total * inverse_first * projected_one
    residual_grad = (
        grad_one + jnp.where(stored[None, :], grad_first - grad_pad_first[:, None], 0.0)
    ).astype(jnp.bfloat16)
    (
        input_weight_grad,
        input_bias_grad,
        output_weight_grad,
        output_bias_grad,
        gain_one_grad,
        gain_two_grad,
        expand_weight_grad,
        expand_bias_grad,
        reduce_weight_grad,
        reduce_bias_grad,
        square_total,
    ) = lax.psum(
        (
            input_weight_grad,
            input_bias_grad,
            output_weight_grad,
            output_bias_grad,
            gain_one_grad,
            gain_two_grad,
            expand_weight_grad,
            expand_bias_grad,
            reduce_weight_grad,
            reduce_bias_grad,
            square_part,
        ),
        "dp",
    )
    residual_rms = jnp.sqrt(square_total / (D * live_count.astype(jnp.float32)))
    return (
        residual_out,
        residual_grad,
        input_weight_grad,
        input_bias_grad,
        output_weight_grad,
        output_bias_grad,
        gain_one_grad,
        gain_two_grad,
        expand_weight_grad,
        expand_bias_grad,
        reduce_weight_grad,
        reduce_bias_grad,
        residual_rms,
        live_count,
    )


def solution(mesh):
    return jax.shard_map(
        on_device,
        mesh=mesh,
        in_specs=(
            P("dp", "mp"),
            P("dp", None),
            P("mp"),
            P(None, None, "mp"),
            P(None, "mp"),
            P("mp", None),
            P("mp"),
            P("mp"),
            P(None, "mp"),
            P("mp"),
            P("mp", None),
            P("mp"),
            P("dp", "mp"),
        ),
        out_specs=(
            P("dp", "mp"),
            P("dp", "mp"),
            P(None, None, "mp"),
            P(None, "mp"),
            P("mp", None),
            P("mp"),
            P("mp"),
            P("mp"),
            P(None, "mp"),
            P("mp"),
            P("mp", None),
            P("mp"),
            P(),
            P(),
        ),
        check_vma=False,
    )
```

profile of v0, /device:TPU:0, one launch (start us, length us, event | category | flops | bytes accessed | tf_op | source)
XLA Modules:
  0.0 926.3 jit_solution(2679985542805380478)
XLA Ops:
  9.9 12.7 %all-reduce.5 = (f32[2048]{0:T(1024)S(1)}, f32[2048]{0:T(1024)S(1)}) all-reduce(f32[2048]{0:T(1024)S(1)} %get-tuple-element.593, f32[2048]{0:T(1024)S(1)} %get-tuple-element.592), channel_id=1, replica_groups=mesh['dp'=8,'mp'=4] {'mp'}, use_global_device_ids=true, to_apply=%region_5.6 | all-reduce | flops 4096 | bytes 32768 | tf_op jit(solution)/shard_map/psum | solution.py:43
  27.5 27.2 %all-gather.5.cloned.1.call-done = bf16[2048,768]{0,1:T(8,128)(2,1)} async-done(((bf16[2048,192]{0,1:T(8,128)(2,1)}), bf16[2048,768]{0,1:T(8,128)(2,1)}) %all-gather.5.cloned.1.call-update) | async-done | bytes 3145744 | tf_op jit(solution)/shard_map/all_gather | solution.py:47
  59.4 94.8 %while.38 = (s32[]{:T(128)}, bf16[4,512,3,64]{1,3,2,0:T(8,128)(2,1)}, f32[4,3,512]{2,1,0:T(4,128)}, s32[4]{0:T(128)S(1)}, s32[2048]{0:T(1024)S(1)}, /*index=5*/p...) while((s32[]{:T(128)}, ...), condition=%wide.region_9.10_spmd, body=%wide.region_6.9_spmd.sunk | while | flops 849445888 | bytes 43996932 | solution.py:102
  62.4 6.0 fusion.149
  68.4 6.8 fusion.150
  75.2 7.3 fusion.151
  86.1 6.0 fusion.149
  92.1 6.8 fusion.150
  98.9 7.3 fusion.151
  109.8 6.0 fusion.149
  115.8 6.8 fusion.150
  122.6 7.3 fusion.151
  133.5 6.0 fusion.149
  139.5 6.8 fusion.150
  146.2 7.3 fusion.151
  161.1 58.5 %reduce-scatter.5.cloned.1.call-done = f32[2048,192]{0,1:T(8,128)} async-done(((f32[2048,768]{0,1:T(8,128)}), f32[2048,192]{0,1:T(8,128)}) %reduce-scatter.5.cloned.1.call-update) | async-done | bytes 1572880 | tf_op jit(solution)/shard_map/reduce_scatter | solution.py:52
  221.7 6.8 psum.184
  233.5 11.0 %all-reduce.4 = (f32[2048]{0:T(1024)}, f32[2048]{0:T(1024)}, f32[2048]{0:T(1024)}) all-reduce(f32[2048]{0:T(1024)} %get-tuple-element.588, f32[2048]{0:T(1024)} %get-tuple-element.587, f32[2048]{0:T(1024)S(1)} %copy-done.36), channel_id=1, replica_groups=mesh['dp'=8,'mp'=4] {'mp'}, use_global_device_ids=true, to_apply=%region_16.17 | all-reduce | flops 6144 | bytes 49152 | tf_op jit(solution)/shard_map/psum | solution.py:43
  251.6 27.4 %all-gather.7.cloned.1.call-done = bf16[2048,768]{0,1:T(8,128)(2,1)} async-done(((bf16[2048,192]{0,1:T(8,128)(2,1)}), bf16[2048,768]{0,1:T(8,128)(2,1)}) %all-gather.7.cloned.1.call-update) | async-done | bytes 3145744 | tf_op jit(solution)/shard_map/all_gather | solution.py:47
  279.0 7.5 fusion.95
  286.5 23.1 %all-gather.9.cloned.1.call-done = bf16[2048,768]{0,1:T(8,128)(2,1)} async-done(((bf16[2048,192]{0,1:T(8,128)(2,1)}), bf16[2048,768]{0,1:T(8,128)(2,1)}) %all-gather.9.cloned.1.call-update) | async-done | bytes 3145744 | tf_op jit(solution)/shard_map/all_gather | solution.py:58
  309.6 12.7 %convert_reduce_fusion = (f32[768]{0:T(1024)}, bf16[2048,768]{1,0:T(8,128)(2,1)S(1)}, bf16[2048,768]{1,0:T(8,128)(2,1)}) fusion(f32[2048,768]{1,0:T(8,128)} %fusion.95, f32[768]{0:T(1024)} %param.26, bf16[2048,768]{0,1:T(8,128)(2,1)} %all-gather.9.cloned.1.call-done, bf16[768,768]{1,0:T(8,128)(2,1)S(1)} %copy-done), kind=kOutput, calls=%fused_computation.58 | convolution fusion | flops 2455239936 | bytes 16914432 | tf_op jit(solution)/shard_map/td,fd->tf/dot_general | solution.py:217
  328.1 6.5 fusion.96
  334.8 31.4 %reduce-scatter.9.cloned.1.call-done = bf16[2048,192]{0,1:T(8,128)(2,1)} async-done(((bf16[2048,768]{0,1:T(8,128)(2,1)}), bf16[2048,192]{0,1:T(8,128)(2,1)}) %reduce-scatter.9.cloned.1.call-update) | async-done | bytes 786448 | tf_op jit(solution)/shard_map/reduce_scatter | solution.py:62
  369.5 57.5 %reduce-scatter.7.cloned.1.call-done = f32[2048,192]{0,1:T(8,128)} async-done(((f32[2048,768]{0,1:T(8,128)}), f32[2048,192]{0,1:T(8,128)}) %reduce-scatter.7.cloned.1.call-update) | async-done | bytes 1572880 | tf_op jit(solution)/shard_map/reduce_scatter | solution.py:52
  428.6 10.3 %all-reduce.3 = (f32[2048]{0:T(1024)S(1)}, f32[2048]{0:T(1024)S(1)}, f32[2048]{0:T(1024)S(1)}, f32[2048]{0:T(1024)S(1)}) all-reduce(f32[2048]{0:T(1024)S(1)} %add_reduce_fusion, f32[2048]{0:T(1024)S(1)} %get-tuple-element.582, f32[2048]{0:T(1024)S(1)} %get-tuple-element.590, ...), channel_id=1, replica_groups=mesh['dp'=8,'mp'=4] {'mp'}, use_global_device_ids=true, to_apply=%region_19.20 | all-reduce | flops 8192 | bytes 65536 | tf_op jit(solution)/shard_map/psum | solution.py:75
  446.1 29.7 %all-gather.11.cloned.1.call-done = bf16[2048,768]{0,1:T(8,128)(2,1)} async-done(((bf16[2048,192]{0,1:T(8,128)(2,1)}), bf16[2048,768]{0,1:T(8,128)(2,1)}) %all-gather.11.cloned.1.call-update) | async-done | bytes 3145744 | tf_op jit(solution)/shard_map/all_gather | solution.py:58
  479.5 144.6 %while.39 = (s32[]{:T(128)}, bf16[2048,3,64]{0,2,1:T(8,128)(2,1)}, f32[2048,3,64]{0,2,1:T(8,128)}, f32[2048,3,64]{0,2,1:T(8,128)}, s32[2048]{0:T(1024)S(1)}, /*i...) while((s32[]{:T(128)}, bf16[2048,3,64]{0,2,1:T(8,128)(2,1)}, ...), condition=%wide.region_31.32_spmd.clone, body=%wide.region_29.31_spmd.clone.sunk | while | flops 2068808704 | bytes 156712976 | solution.py:146
  500.1 5.8 multiply_reduce_fusion.5
  505.8 6.1 multiply_convert_fusion.5
  511.9 5.8 fusion.162
  527.6 6.1 fusion.164
  533.7 5.8 multiply_reduce_fusion.5
  539.4 6.1 multiply_convert_fusion.5
  545.6 5.8 fusion.162
  561.8 6.1 fusion.164
  567.8 5.8 multiply_reduce_fusion.5
  573.6 6.1 multiply_convert_fusion.5
  579.7 5.8 fusion.162
  595.9 6.1 fusion.164
  607.8 6.1 multiply_convert_fusion.5
  613.9 5.8 fusion.162
  630.6 7.0 fusion.99
  648.2 12.0 %psum.207 = s32[]{:T(128)} all-reduce(s32[]{:T(128)} %reduce_sum.273), channel_id=1, replica_groups=mesh['dp'=8,'mp'=4] {'dp'}, use_global_device_ids=true, to_apply=%region_61.62 | all-reduce | flops 1 | bytes 8 | tf_op jit(solution)/shard_map/psum | solution.py:168
  662.4 6.2 reduce-scatter.11.cloned.1.call-done
  671.0 10.3 %all-reduce.2 = (f32[2048]{0:T(1024)S(1)}, f32[2048]{0:T(1024)S(1)}, f32[2048]{0:T(1024)S(1)}, f32[2048]{0:T(1024)S(1)}) all-reduce(f32[2048]{0:T(1024)S(1)} %get-tuple-element.584, f32[2048]{0:T(1024)S(1)} %get-tuple-element.589, f32[2048]{0:T(1024)S(1)} %copy-done.37, f32[2048]{0:T(1024)S(1)} %copy-done.38), channel_id=1, replica_groups=mesh['dp'=8,'mp'=4] {'mp'}, use_global_device_ids=true, to_apply=%region_34.35 | all-reduce | flops 8192 | bytes 65536 | tf_op jit(solution)/shard_map/psum | solution.py:282
  682.5 39.7 %all-reduce = (f32[2,192]{1,0:T(2,128)}, f32[192]{0:T(256)}, f32[192]{0:T(256)}, f32[192]{0:T(256)}, f32[768]{0:T(1024)}, /*index=5*/f32[192]{0:T(256)}, f32[]{:T(128)}) all-reduce(f32[2,192]{1,0:T(2,128)S(1)} %pad_maximum_fusion.3, f32[192]{0:T(256)S(1)} %copy-done.52, ...), channel_id=1, replica_groups=mesh['dp'=8,'mp'=4] {'dp'}, use_global_device_ids=true, to_apply=%region_40.41 | all-reduce | flops 1921 | bytes 15368 | tf_op jit(solution)/shard_map/psum | solution.py:309
  726.0 184.6 %all-reduce.8.cloned.1.call-done = (f32[3,768,192]{1,2,0:T(8,128)}, f32[192,768]{1,0:T(8,128)}, f32[768,768]{1,0:T(8,128)}, f32[768,768]{1,0:T(8,128)}) async-done(((f32[3,768,192]{1,2,0:T(8,128)}, f32[192,768]{1,0:T(8,128)}, f32[768,768]{1,0:T(8,128)}, f32[768,768]{1,0:T(8,128)}), (f32[3,768,192]{1,2,0:T(8,128)}, f32[192,768]{1,0:T(8,128)}, f32[768,768]{1,0:T(8,128)}, ...) | async-done | bytes 7077904 | tf_op jit(solution)/shard_map/psum | solution.py:309
  (321 shorter events, 150.4 us)
Async XLA Ops:
  7.2 302.5 %copy-start = (bf16[768,768]{1,0:T(8,128)(2,1)S(1)}, bf16[768,768]{1,0:T(8,128)(2,1)}, u32[]{:S(2)}) copy-start(bf16[768,768]{1,0:T(8,128)(2,1)} %param.27) | copy-start | bytes 3538948
  7.2 18.5 %copy-start.63 = (s32[1,4]{1,0:T(1,128)S(1)}, s32[1,4]{1,0:T(1,128)}, u32[]{:S(2)}) copy-start(s32[1,4]{1,0:T(1,128)} %param.18) | copy-start | bytes 52
  7.2 19.3 %copy-start.57 = (f32[2,192]{1,0:T(2,128)S(1)}, f32[2,192]{1,0:T(2,128)}, u32[]{:S(2)}) copy-start(f32[2,192]{1,0:T(2,128)} %param.21) | copy-start | bytes 4612
  7.2 47.5 %copy-start.61 = (bf16[3,768,192]{1,2,0:T(8,128)(2,1)S(1)}, bf16[3,768,192]{1,2,0:T(8,128)(2,1)}, u32[]{:S(2)}) copy-start(bf16[3,768,192]{1,2,0:T(8,128)(2,1)} %param.20) | copy-start | bytes 2654212
  7.2 47.4 %all-gather.5.cloned.1.call-start = ((), (), s32[]{:S(2)}) async-start(), calls=%async_computation.4 | async-start | bytes 3932160 | tf_op jit(solution)/shard_map/all_gather | solution.py:47
  7.3 51.3 %copy-start.43 = (pred[192]{0:T(512)(128)(4,1)}, pred[192]{0:T(512)(128)(4,1)S(1)}, u32[]{:S(2)}) copy-start(pred[192]{0:T(512)(128)(4,1)S(1)} %get-tuple-element.690) | copy-start | bytes 580
  7.3 51.3 %copy-start.46 = (pred[192]{0:T(512)(128)(4,1)}, pred[192]{0:T(512)(128)(4,1)S(1)}, u32[]{:S(2)}) copy-start(pred[192]{0:T(512)(128)(4,1)S(1)} %get-tuple-element.689) | copy-start | bytes 580
  22.6 36.0 %copy-start.41 = (f32[2048]{0:T(1024)}, f32[2048]{0:T(1024)S(1)}, u32[]{:S(2)}) copy-start(f32[2048]{0:T(1024)S(1)} %get-tuple-element.661) | copy-start | bytes 24580
  25.7 193.9 %reduce-scatter.5.cloned.1.call-start = ((), (), s32[]{:S(2)}) async-start(), calls=%async_computation.5 | async-start | bytes 7864320 | tf_op jit(solution)/shard_map/reduce_scatter | solution.py:52
  154.2 6.8 copy-start.56
  161.0 58.5 %copy-start.54 = (f32[192]{0:T(256)S(1)}, f32[192]{0:T(256)}, u32[]{:S(2)}) copy-start(f32[192]{0:T(256)} %param.23) | copy-start | bytes 2308
  161.0 68.2 %copy-start.9 = (bf16[2048,192]{0,1:T(8,128)(2,1)S(1)}, bf16[2048,192]{0,1:T(8,128)(2,1)}, u32[]{:S(2)}) copy-start(bf16[2048,192]{0,1:T(8,128)(2,1)} %param.17) | copy-start | bytes 2359300
  161.0 118.0 %all-gather.7.cloned.1.call-start = ((), (), s32[]{:S(2)}) async-start(), calls=%async_computation.6 | async-start | bytes 3932160 | tf_op jit(solution)/shard_map/all_gather | solution.py:47
  221.7 11.7 %copy-start.36 = (f32[2048]{0:T(1024)S(1)}, f32[2048]{0:T(1024)}, u32[]{:S(2)}) copy-start(f32[2048]{0:T(1024)} %get-tuple-element.597) | copy-start | bytes 24580
  233.4 16.3 %copy-start.14 = (bf16[2048,192]{0,1:T(8,128)(2,1)S(1)}, bf16[2048,192]{0,1:T(8,128)(2,1)}, u32[]{:S(2)}) copy-start(bf16[2048,192]{0,1:T(8,128)(2,1)} %param.29) | copy-start | bytes 2359300
  248.4 61.2 %all-gather.9.cloned.1.call-start = ((), (), s32[]{:S(2)}) async-start(), calls=%async_computation.8 | async-start | bytes 3932160 | tf_op jit(solution)/shard_map/all_gather | solution.py:58
  251.6 114.6 %reduce-scatter.9.cloned.1.call-start = ((), (), s32[]{:S(2)}) async-start(), calls=%async_computation.9 | async-start | bytes 3932160 | tf_op jit(solution)/shard_map/reduce_scatter | solution.py:62
  309.6 14.4 %copy-start.60 = (bf16[768,768]{1,0:T(8,128)(2,1)S(1)}, bf16[768,768]{1,0:T(8,128)(2,1)}, u32[]{:S(2)}) copy-start(bf16[768,768]{1,0:T(8,128)(2,1)} %param.25) | copy-start | bytes 3538948
  328.1 98.9 %reduce-scatter.7.cloned.1.call-start = ((), (), s32[]{:S(2)}) async-start(), calls=%async_computation.7 | async-start | bytes 7864320 | tf_op jit(solution)/shard_map/reduce_scatter | solution.py:52
  334.6 31.5 %copy-start.33 = (f32[2048]{0:T(1024)S(1)}, f32[2048]{0:T(1024)}, u32[]{:S(2)}) copy-start(f32[2048]{0:T(1024)} %copy-done.32) | copy-start | bytes 24580
  334.6 31.5 %copy-start.47 = (pred[192]{0:T(512)(128)(4,1)S(1)}, pred[192]{0:T(512)(128)(4,1)}, u32[]{:S(2)}) copy-start(pred[192]{0:T(512)(128)(4,1)} %copy-done.46) | copy-start | bytes 580
  334.6 31.5 %copy-start.49 = (f32[192]{0:T(256)S(1)}, f32[192]{0:T(256)}, u32[]{:S(2)}) copy-start(f32[192]{0:T(256)} %param.24) | copy-start | bytes 2308
  334.7 92.3 %copy-start.55 = (f32[192]{0:T(256)S(1)}, f32[192]{0:T(256)}, u32[]{:S(2)}) copy-start(f32[192]{0:T(256)} %param.28) | copy-start | bytes 2308
  334.7 104.2 %copy-start.39 = (f32[2048]{0:T(1024)S(1)}, f32[2048]{0:T(1024)}, u32[]{:S(2)}) copy-start(f32[2048]{0:T(1024)} %get-tuple-element.659) | copy-start | bytes 24580
  334.7 104.2 %copy-start.40 = (f32[2048]{0:T(1024)S(1)}, f32[2048]{0:T(1024)}, u32[]{:S(2)}) copy-start(f32[2048]{0:T(1024)} %get-tuple-element.658) | copy-start | bytes 24580
  334.7 104.2 %copy-start.44 = (pred[192]{0:T(512)(128)(4,1)S(1)}, pred[192]{0:T(512)(128)(4,1)}, u32[]{:S(2)}) copy-start(pred[192]{0:T(512)(128)(4,1)} %copy-done.43) | copy-start | bytes 580
  334.7 141.1 %all-gather.11.cloned.1.call-start = ((), (), s32[]{:S(2)}) async-start(), calls=%async_computation.10 | async-start | bytes 3932160 | tf_op jit(solution)/shard_map/all_gather | solution.py:58
  366.2 72.8 %copy-start.21 = (bf16[2048,192]{0,1:T(8,128)(2,1)S(1)}, bf16[2048,192]{0,1:T(8,128)(2,1)}, u32[]{:S(2)}) copy-start(bf16[2048,192]{0,1:T(8,128)(2,1)} %reduce-scatter.9.cloned.1.call-done) | copy-start | bytes 2359300
  443.8 32.0 %copy-start.26 = (bf16[192,768]{1,0:T(8,128)(2,1)S(1)}, bf16[192,768]{1,0:T(8,128)(2,1)}, u32[]{:S(2)}) copy-start(bf16[192,768]{1,0:T(8,128)(2,1)} %param.22) | copy-start | bytes 884740
  446.1 222.5 %reduce-scatter.11.cloned.1.call-start = ((), (), s32[]{:S(2)}) async-start(), calls=%async_computation.11 | async-start | bytes 3932160 | tf_op jit(solution)/shard_map/reduce_scatter | solution.py:62
  630.5 280.1 %all-reduce.8.cloned.1.call-start = ((), (), s32[]{:S(2)}) async-start(), calls=%async_computation.12 | async-start | bytes 14155776 | tf_op jit(solution)/shard_map/psum | solution.py:309
  630.5 7.1 copy-start.59
  630.6 7.1 copy-start.66
  646.9 21.7 %copy-start.10 = (bf16[2048,192]{0,1:T(8,128)(2,1)S(1)}, bf16[2048,192]{0,1:T(8,128)(2,1)}, u32[]{:S(2)}) copy-start(bf16[2048,192]{0,1:T(8,128)(2,1)} %param.17) | copy-start | bytes 2359300
  646.9 21.7 %copy-start.15 = (bf16[2048,192]{0,1:T(8,128)(2,1)S(1)}, bf16[2048,192]{0,1:T(8,128)(2,1)}, u32[]{:S(2)}) copy-start(bf16[2048,192]{0,1:T(8,128)(2,1)} %param.29) | copy-start | bytes 2359300
  646.9 21.7 %copy-start.29 = (f32[2048]{0:T(1024)S(1)}, f32[2048]{0:T(1024)}, u32[]{:S(2)}) copy-start(f32[2048]{0:T(1024)} %copy-done.28) | copy-start | bytes 24580
  646.9 21.7 %copy-start.31 = (f32[2048]{0:T(1024)S(1)}, f32[2048]{0:T(1024)}, u32[]{:S(2)}) copy-start(f32[2048]{0:T(1024)} %copy-done.30) | copy-start | bytes 24580
  646.9 21.7 %copy-start.35 = (f32[2048]{0:T(1024)S(1)}, f32[2048]{0:T(1024)}, u32[]{:S(2)}) copy-start(f32[2048]{0:T(1024)} %copy-done.34) | copy-start | bytes 24580
  646.9 21.7 %copy-start.45 = (pred[192]{0:T(512)(128)(4,1)S(1)}, pred[192]{0:T(512)(128)(4,1)}, u32[]{:S(2)}) copy-start(pred[192]{0:T(512)(128)(4,1)} %copy-done.43) | copy-start | bytes 580
  646.9 21.7 %copy-start.48 = (pred[192]{0:T(512)(128)(4,1)S(1)}, pred[192]{0:T(512)(128)(4,1)}, u32[]{:S(2)}) copy-start(pred[192]{0:T(512)(128)(4,1)} %copy-done.46) | copy-start | bytes 580
  646.9 21.7 %copy-start.50 = (f32[192]{0:T(256)S(1)}, f32[192]{0:T(256)}, u32[]{:S(2)}) copy-start(f32[192]{0:T(256)} %param.19) | copy-start | bytes 2308
  647.6 23.4 %copy-start.37 = (f32[2048]{0:T(1024)S(1)}, f32[2048]{0:T(1024)}, u32[]{:S(2)}) copy-start(f32[2048]{0:T(1024)} %get-tuple-element.679) | copy-start | bytes 24580
  647.6 23.4 %copy-start.38 = (f32[2048]{0:T(1024)S(1)}, f32[2048]{0:T(1024)}, u32[]{:S(2)}) copy-start(f32[2048]{0:T(1024)} %get-tuple-element.680) | copy-start | bytes 24580
  647.6 35.0 %copy-start.51 = (f32[192]{0:T(256)S(1)}, f32[192]{0:T(256)}, u32[]{:S(2)}) copy-start(f32[192]{0:T(256)} %get-tuple-element.581) | copy-start | bytes 2308
  647.6 35.0 %copy-start.52 = (f32[192]{0:T(256)S(1)}, f32[192]{0:T(256)}, u32[]{:S(2)}) copy-start(f32[192]{0:T(256)} %get-tuple-element.664) | copy-start | bytes 2308
  647.6 35.0 %copy-start.53 = (f32[768]{0:T(1024)S(1)}, f32[768]{0:T(1024)}, u32[]{:S(2)}) copy-start(f32[768]{0:T(1024)} %get-tuple-element.662) | copy-start | bytes 9220
  647.6 75.4 %copy-start.42 = (f32[2048]{0:T(1024)S(1)}, f32[2048]{0:T(1024)}, u32[]{:S(2)}) copy-start(f32[2048]{0:T(1024)} %copy-done.41) | copy-start | bytes 24580
  647.6 75.4 %copy-start.12 = (f32[2048,192]{0,1:T(8,128)S(1)}, f32[2048,192]{0,1:T(8,128)}, u32[]{:S(2)}) copy-start(f32[2048,192]{0,1:T(8,128)} %copy-done.11) | copy-start | bytes 4718596
  (52 other events, 204.2 us)
Sparse Core Ops, SparseCore 0:
  25.8 28.8 all-gather.4
  161.2 58.3 reduce-scatter.4
  248.5 30.4 all-gather.6
  281.1 28.5 all-gather.8
  328.2 37.9 reduce-scatter.8
  368.6 58.3 reduce-scatter.6
  446.2 29.5 all-gather.10
  630.6 37.9 reduce-scatter.10
  674.2 236.3 all-reduce.7
where the time goes:
time: 936 us; the launch traced here: 926 us
  waiting for transfers between devices  446 us (48%)
  matrix products  212 us (23%)
  other arithmetic  107 us (11%)
  blocking collectives  103 us (11%)
  local copies, waits for them, and re-layouts  28.5 us (3%)
  between operations  17.3 us (2%)
  loops' own time  13 us (1%)
    psum x1, waiting for transfers between devices, on_device(): lax.psum((input_weight_grad, input_bias_grad, output_weight_grad, output_...  185 us
    reduce_scatter x2, waiting for transfers between devices, sum_branch(): lax.psum_scatter(partial_rows, 'mp', scatter_dimension=1, tiled=True)  116 us
    all_gather x2, waiting for transfers between devices, gather_normed(): return lax.all_gather(normed, 'mp', axis=1, tiled=True)  54.6 us
    all_gather x2, waiting for transfers between devices, spread_grads(): return lax.all_gather(grad_rows, 'mp', axis=1, tiled=True)  52.8 us
    psum x1, blocking collectives, on_device(): lax.psum((input_weight_grad, input_bias_grad, output_weight_grad, output_...  39.7 us
    reduce_scatter x2, waiting for transfers between devices, feature_sums(): lax.psum_scatter(partial_rows.astype(jnp.bfloat16), 'mp', scatter_dimensi...  37.6 us
    dot_general x4, matrix products, attend_block(): jnp.einsum('hqk,khd->qhd', attn_probs, value_rows, preferred_element_type...  29.3 us
    reduce_sum x4, other arithmetic, attend_block(): row_sum = jnp.sum(weights, axis=2, keepdims=True)  27.1 us
  transfers between devices with their start and end apart: 9, of which 9 were waited for; matrix products, arithmetic and copies ran while one was open for 5% of the time, Pallas kernels for 0%

commit v1 on v0

--- a/solution.py
+++ b/solution.py
@@ -44,7 +44,29 @@
 
 
 def gather_normed(normed):
-    return lax.all_gather(normed, "mp", axis=1, tiled=True)
+
+    def _mix_panels(z_in):
+        long_array, placed, parts_out = (lax.psum(1, "mp"), lax.axis_index("mp"), z_in.shape[1])
+        store = list(map(lambda s: (s, (s + 1) % long_array), range(long_array)))
+        z2 = range(long_array)
+        sheets = list(map(lambda s: (s, (s - 1) % long_array), z2))
+        finding = jnp.zeros((*z_in.shape[:1], long_array * parts_out, *z_in.shape[2:]), z_in.dtype)
+        state_next = value_now = z_in
+        finding = lax.dynamic_update_slice_in_dim(finding, z_in, placed * parts_out, axis=1)
+        t1 = long_array // 2
+        for at in range(1, t1 + 1):
+            state_next = lax.ppermute(state_next, axis_name="mp", perm=store)
+            finding = lax.dynamic_update_slice_in_dim(
+                finding, state_next, (placed - at) % long_array * parts_out, axis=1
+            )
+            if at < long_array - t1:
+                value_now = lax.ppermute(value_now, "mp", sheets)
+                finding = lax.dynamic_update_slice_in_dim(
+                    finding, value_now, (placed + at) % long_array * parts_out, axis=1
+                )
+        return finding
+
+    return _mix_panels(normed)
 
 
 def sum_branch(partial_rows, bias_vec):

time: 936 us -> 998 us (1.066)
  local copies, waits for them, and re-layouts: 28.5 us -> 131 us
  waiting for transfers between devices: 446 us -> 410 us
  starting transfers between devices: 0.37 us -> 11 us
    dynamic_update_slice x0 -> x8, local copies, waits for them, and re-layouts: none -> 86.2 us  [the longest x4 42.2 us: _mix_panels(): lax.dynamic_update_slice_in_dim(finding, state_next, (placed - at) % long...]
    all_gather x2 -> x0, waiting for transfers between devices: 54.6 us -> none  [gather_normed(): return lax.all_gather(normed, 'mp', axis=1, tiled=True)]
    ppermute x0 -> x6, waiting for transfers between devices: none -> 39.9 us  [the longest x4 39.9 us: _mix_panels(): state_next = lax.ppermute(state_next, axis_name='mp', perm=store)]
    all_gather x2, waiting for transfers between devices: 52.8 us -> 29.7 us  [spread_grads(): return lax.all_gather(grad_rows, 'mp', axis=1, tiled=True)]
    ppermute x0 -> x6, local copies, waits for them, and re-layouts: none -> 10.9 us  [the longest x4 7.29 us: _mix_panels(): state_next = lax.ppermute(state_next, axis_name='mp', perm=store)]
    ppermute x0 -> x6, starting transfers between devices: none -> 10.3 us  [the longest x4 7.49 us: _mix_panels(): state_next = lax.ppermute(state_next, axis_name='mp', perm=store)]
  transfers between devices with their start and end apart: 9 -> 13, of which waited for: 9 -> 8; matrix products, arithmetic and copies ran while one was open for 5% -> 13% of each run, Pallas kernels for 0% -> 0%
where the time goes in v1:
time: 998 us; the launch traced here: 984 us
  waiting for transfers between devices  410 us (41%)
  matrix products  205 us (21%)
  local copies, waits for them, and re-layouts  131 us (13%)
  other arithmetic  104 us (10%)
  blocking collectives  102 us (10%)
  between operations  17.8 us (2%)
  starting transfers between devices  11 us (1%)
    psum x1, waiting for transfers between devices, on_device(): lax.psum((input_weight_grad, input_bias_grad, output_weight_grad, output_...  185 us
    reduce_scatter x2, waiting for transfers between devices, sum_branch(): lax.psum_scatter(partial_rows, 'mp', scatter_dimension=1, tiled=True)  117 us
    dynamic_update_slice x4, local copies, waits for them, and re-layouts, _mix_panels(): lax.dynamic_update_slice_in_dim(finding, state_next, (placed - at) % long...  42.2 us
    ppermute x4, waiting for transfers between devices, _mix_panels(): state_next = lax.ppermute(state_next, axis_name='mp', perm=store)  39.9 us
    psum x1, blocking collectives, on_device(): lax.psum((input_weight_grad, input_bias_grad, output_weight_grad, output_...  39.7 us
    reduce_scatter x2, waiting for transfers between devices, feature_sums(): lax.psum_scatter(partial_rows.astype(jnp.bfloat16), 'mp', scatter_dimensi...  38.8 us
    all_gather x2, waiting for transfers between devices, spread_grads(): return lax.all_gather(grad_rows, 'mp', axis=1, tiled=True)  29.7 us
    dot_general x4, matrix products, attend_block(): jnp.einsum('hqk,khd->qhd', attn_probs, value_rows, preferred_element_type...  29.3 us
  transfers between devices with their start and end apart: 13, of which 8 were waited for; matrix products, arithmetic and copies ran while one was open for 13% of the time, Pallas kernels for 0%

profile of v1, /device:TPU:0, one launch (start us, length us, event | category | flops | bytes accessed | tf_op | source)
XLA Modules:
  0.0 984.5 jit_solution(6832550262938993240)
XLA Ops:
  9.9 12.7 %all-reduce.5 = (f32[2048]{0:T(1024)S(1)}, f32[2048]{0:T(1024)S(1)}) all-reduce(f32[2048]{0:T(1024)S(1)} %get-tuple-element.593, f32[2048]{0:T(1024)S(1)} %get-tuple-element.592), channel_id=1, replica_groups=mesh['dp'=8,'mp'=4] {'mp'}, use_global_device_ids=true, to_apply=%region_5.6 | all-reduce | flops 4096 | bytes 32768 | tf_op jit(solution)/shard_map/psum | solution.py:43
  25.9 17.5 %collective-permute-done = bf16[2048,192]{0,1:T(8,128)(2,1)} collective-permute-done((bf16[2048,192]{0,1:T(8,128)(2,1)S(1)}, bf16[2048,192]{0,1:T(8,128)(2,1)}, u32[]{:S(2)}, u32[]{:S(2)}) %collective-permute-start) | collective-permute-done | bytes 786464 | tf_op jit(solution)/shard_map/ppermute | solution.py:58
  46.9 10.2 %dynamic_update_slice.57 = bf16[2048,768]{1,0:T(8,128)(2,1)} dynamic-update-slice(bf16[2048,768]{1,0:T(8,128)(2,1)} %broadcast.387.clone, bf16[2048,192]{1,0:T(8,128)(2,1)S(1)} %copy.44, s32[]{:T(128)} %constant.254.clone.1, s32[]{:T(128)S(6)} %select_n.135) | dynamic-update-slice | bytes 1572868 | tf_op jit(solution)/shard_map/dynamic_update_slice | solution.py:55
  59.2 10.7 %dynamic_update_slice.58 = bf16[2048,768]{1,0:T(8,128)(2,1)} dynamic-update-slice(bf16[2048,768]{1,0:T(8,128)(2,1)} %dynamic_update_slice.57, bf16[2048,192]{1,0:T(8,128)(2,1)S(1)} %copy.45, s32[]{:T(128)} %constant.254.clone.1, s32[]{:T(128)S(6)} %select_n.137) | dynamic-update-slice | bytes 1572868 | tf_op jit(solution)/shard_map/dynamic_update_slice | solution.py:59
  71.3 11.4 %dynamic_update_slice.59 = bf16[2048,768]{1,0:T(8,128)(2,1)} dynamic-update-slice(bf16[2048,768]{1,0:T(8,128)(2,1)} %dynamic_update_slice.58, bf16[2048,192]{1,0:T(8,128)(2,1)S(1)} %copy.46, s32[]{:T(128)} %constant.254.clone.1, s32[]{:T(128)S(6)} %select_n.139) | dynamic-update-slice | bytes 1572868 | tf_op jit(solution)/shard_map/dynamic_update_slice | solution.py:64
  84.2 9.9 %dynamic_update_slice.60 = bf16[2048,768]{1,0:T(8,128)(2,1)} dynamic-update-slice(bf16[2048,768]{1,0:T(8,128)(2,1)} %dynamic_update_slice.59, bf16[2048,192]{1,0:T(8,128)(2,1)S(1)} %copy.47, s32[]{:T(128)} %constant.254.clone.1, s32[]{:T(128)S(6)} %select_n.141) | dynamic-update-slice | bytes 1572868 | tf_op jit(solution)/shard_map/dynamic_update_slice | solution.py:59
  99.0 94.8 %while.38 = (s32[]{:T(128)}, bf16[4,512,3,64]{1,3,2,0:T(8,128)(2,1)}, f32[4,3,512]{2,1,0:T(4,128)}, s32[4]{0:T(128)S(1)}, s32[2048]{0:T(1024)S(1)}, /*index=5*/p...) while((s32[]{:T(128)}, ...), condition=%wide.region_9.10_spmd, body=%wide.region_6.9_spmd.sunk | while | flops 849445888 | bytes 43996932 | solution.py:124
  102.1 6.0 fusion.149
  108.0 6.8 fusion.150
  114.8 7.3 fusion.151
  125.7 6.0 fusion.149
  131.7 6.8 fusion.150
  138.5 7.3 fusion.151
  149.4 6.0 fusion.149
  155.4 6.8 fusion.150
  162.2 7.3 fusion.151
  173.1 6.0 fusion.149
  179.1 6.8 fusion.150
  185.9 7.3 fusion.151
  201.0 59.5 %reduce-scatter.5.cloned.1.call-done = f32[2048,192]{0,1:T(8,128)} async-done(((f32[2048,768]{0,1:T(8,128)}), f32[2048,192]{0,1:T(8,128)}) %reduce-scatter.5.cloned.1.call-update) | async-done | bytes 1572880 | tf_op jit(solution)/shard_map/reduce_scatter | solution.py:74
  262.8 6.5 psum.184
  274.2 10.3 %all-reduce.4 = (f32[2048]{0:T(1024)S(1)}, f32[2048]{0:T(1024)S(1)}, f32[2048]{0:T(1024)S(1)}) all-reduce(f32[2048]{0:T(1024)} %get-tuple-element.588, f32[2048]{0:T(1024)} %get-tuple-element.587, f32[2048]{0:T(1024)S(1)} %copy-done.38), channel_id=1, replica_groups=mesh['dp'=8,'mp'=4] {'mp'}, use_global_device_ids=true, to_apply=%region_16.17 | all-reduce | flops 6144 | bytes 49152 | tf_op jit(solution)/shard_map/psum | solution.py:43
  290.5 22.4 %collective-permute-done.3 = bf16[2048,192]{0,1:T(8,128)(2,1)} collective-permute-done((bf16[2048,192]{0,1:T(8,128)(2,1)S(1)}, bf16[2048,192]{0,1:T(8,128)(2,1)}, u32[]{:S(2)}, u32[]{:S(2)}) %collective-permute-start.3) | collective-permute-done | bytes 786464 | tf_op jit(solution)/shard_map/ppermute | solution.py:58
  312.9 6.7 collective-permute-start.5
  322.7 10.5 %dynamic_update_slice.61 = bf16[2048,768]{1,0:T(8,128)(2,1)} dynamic-update-slice(bf16[2048,768]{1,0:T(8,128)(2,1)} %broadcast.387, bf16[2048,192]{1,0:T(8,128)(2,1)} %copy.49, s32[]{:T(128)} %constant.254.clone.1, s32[]{:T(128)S(6)} %select_n.135) | dynamic-update-slice | bytes 1572868 | tf_op jit(solution)/shard_map/dynamic_update_slice | solution.py:55
  335.5 11.2 %dynamic_update_slice.62 = bf16[2048,768]{1,0:T(8,128)(2,1)} dynamic-update-slice(bf16[2048,768]{1,0:T(8,128)(2,1)} %dynamic_update_slice.61, bf16[2048,192]{1,0:T(8,128)(2,1)} %copy.50, s32[]{:T(128)} %constant.254.clone.1, s32[]{:T(128)S(6)} %select_n.137) | dynamic-update-slice | bytes 1572868 | tf_op jit(solution)/shard_map/dynamic_update_slice | solution.py:59
  348.9 11.9 %dynamic_update_slice.63 = bf16[2048,768]{1,0:T(8,128)(2,1)} dynamic-update-slice(bf16[2048,768]{1,0:T(8,128)(2,1)} %dynamic_update_slice.62, bf16[2048,192]{1,0:T(8,128)(2,1)} %copy.51, s32[]{:T(128)} %constant.254.clone.1, s32[]{:T(128)S(6)} %select_n.139) | dynamic-update-slice | bytes 1572868 | tf_op jit(solution)/shard_map/dynamic_update_slice | solution.py:64
  363.0 10.4 %dynamic_update_slice.64 = bf16[2048,768]{1,0:T(8,128)(2,1)} dynamic-update-slice(bf16[2048,768]{1,0:T(8,128)(2,1)} %dynamic_update_slice.63, bf16[2048,192]{1,0:T(8,128)(2,1)} %copy.52, s32[]{:T(128)} %constant.254.clone.1, s32[]{:T(128)S(6)} %select_n.141) | dynamic-update-slice | bytes 1572868 | tf_op jit(solution)/shard_map/dynamic_update_slice | solution.py:59
  378.6 8.6 convert_reduce_fusion
  394.1 6.5 fusion.96
  400.8 32.7 %reduce-scatter.9.cloned.1.call-done = bf16[2048,192]{0,1:T(8,128)(2,1)} async-done(((bf16[2048,768]{0,1:T(8,128)(2,1)}), bf16[2048,192]{0,1:T(8,128)(2,1)}) %reduce-scatter.9.cloned.1.call-update) | async-done | bytes 786448 | tf_op jit(solution)/shard_map/reduce_scatter | solution.py:84
  436.8 57.5 %reduce-scatter.7.cloned.1.call-done = f32[2048,192]{0,1:T(8,128)} async-done(((f32[2048,768]{0,1:T(8,128)}), f32[2048,192]{0,1:T(8,128)}) %reduce-scatter.7.cloned.1.call-update) | async-done | bytes 1572880 | tf_op jit(solution)/shard_map/reduce_scatter | solution.py:74
  495.9 10.3 %all-reduce.3 = (f32[2048]{0:T(1024)S(1)}, f32[2048]{0:T(1024)S(1)}, f32[2048]{0:T(1024)S(1)}, f32[2048]{0:T(1024)S(1)}) all-reduce(f32[2048]{0:T(1024)S(1)} %add_reduce_fusion, f32[2048]{0:T(1024)S(1)} %get-tuple-element.582, f32[2048]{0:T(1024)S(1)} %get-tuple-element.590, ...), channel_id=1, replica_groups=mesh['dp'=8,'mp'=4] {'mp'}, use_global_device_ids=true, to_apply=%region_19.20 | all-reduce | flops 8192 | bytes 65536 | tf_op jit(solution)/shard_map/psum | solution.py:97
  513.4 29.7 %all-gather.5.cloned.1.call-done = bf16[2048,768]{0,1:T(8,128)(2,1)} async-done(((bf16[2048,192]{0,1:T(8,128)(2,1)}), bf16[2048,768]{0,1:T(8,128)(2,1)}) %all-gather.5.cloned.1.call-update) | async-done | bytes 3145744 | tf_op jit(solution)/shard_map/all_gather | solution.py:80
  546.8 135.1 %while.39 = (s32[]{:T(128)}, bf16[2048,3,64]{0,2,1:T(8,128)(2,1)}, f32[2048,3,64]{0,2,1:T(8,128)}, f32[2048,3,64]{0,2,1:T(8,128)}, s32[2048]{0:T(1024)S(1)}, /*i...) while((s32[]{:T(128)}, bf16[2048,3,64]{0,2,1:T(8,128)(2,1)}, ...), condition=%wide.region_31.32_spmd.clone, body=%wide.region_29.31_spmd.clone.sunk | while | flops 2068808704 | bytes 156712976 | solution.py:168
  563.6 6.1 multiply_convert_fusion.5
  585.4 6.1 fusion.164
  597.2 6.1 multiply_convert_fusion.5
  619.6 6.1 fusion.164
  631.4 6.1 multiply_convert_fusion.5
  653.7 6.1 fusion.164
  665.6 6.1 multiply_convert_fusion.5
  688.4 7.1 fusion.99
  706.1 12.0 %psum.207 = s32[]{:T(128)} all-reduce(s32[]{:T(128)} %reduce_sum.273), channel_id=1, replica_groups=mesh['dp'=8,'mp'=4] {'dp'}, use_global_device_ids=true, to_apply=%region_61.62 | all-reduce | flops 1 | bytes 8 | tf_op jit(solution)/shard_map/psum | solution.py:190
  720.3 6.1 reduce-scatter.11.cloned.1.call-done
  728.8 10.3 %all-reduce.2 = (f32[2048]{0:T(1024)S(1)}, f32[2048]{0:T(1024)S(1)}, f32[2048]{0:T(1024)S(1)}, f32[2048]{0:T(1024)S(1)}) all-reduce(f32[2048]{0:T(1024)S(1)} %get-tuple-element.584, f32[2048]{0:T(1024)S(1)} %get-tuple-element.589, f32[2048]{0:T(1024)S(1)} %copy-done.39, f32[2048]{0:T(1024)S(1)} %copy-done.40), channel_id=1, replica_groups=mesh['dp'=8,'mp'=4] {'mp'}, use_global_device_ids=true, to_apply=%region_34.35 | all-reduce | flops 8192 | bytes 65536 | tf_op jit(solution)/shard_map/psum | solution.py:304
  740.3 39.7 %all-reduce = (f32[2,192]{1,0:T(2,128)}, f32[192]{0:T(256)}, f32[192]{0:T(256)}, f32[192]{0:T(256)}, f32[768]{0:T(1024)}, /*index=5*/f32[192]{0:T(256)}, f32[]{:T(128)}) all-reduce(f32[2,192]{1,0:T(2,128)S(1)} %pad_maximum_fusion.3, f32[192]{0:T(256)S(1)} %copy-done.56, ...), channel_id=1, replica_groups=mesh['dp'=8,'mp'=4] {'dp'}, use_global_device_ids=true, to_apply=%region_40.41 | all-reduce | flops 1921 | bytes 15368 | tf_op jit(solution)/shard_map/psum | solution.py:331
  783.7 184.7 %all-reduce.8.cloned.1.call-done = (f32[3,768,192]{1,2,0:T(8,128)}, f32[192,768]{1,0:T(8,128)}, f32[768,768]{1,0:T(8,128)}, f32[768,768]{1,0:T(8,128)}) async-done(((f32[3,768,192]{1,2,0:T(8,128)}, f32[192,768]{1,0:T(8,128)}, f32[768,768]{1,0:T(8,128)}, f32[768,768]{1,0:T(8,128)}), (f32[3,768,192]{1,2,0:T(8,128)}, f32[192,768]{1,0:T(8,128)}, f32[768,768]{1,0:T(8,128)}, ...) | async-done | bytes 7077904 | tf_op jit(solution)/shard_map/psum | solution.py:331
  (351 shorter events, 213.3 us)
Async XLA Ops:
  7.2 371.4 %copy-start = (bf16[768,768]{1,0:T(8,128)(2,1)S(1)}, bf16[768,768]{1,0:T(8,128)(2,1)}, u32[]{:S(2)}) copy-start(bf16[768,768]{1,0:T(8,128)(2,1)} %param.25) | copy-start | bytes 3538948
  7.2 253.4 %reduce-scatter.5.cloned.1.call-start = ((), (), s32[]{:S(2)}) async-start(), calls=%async_computation.4 | async-start | bytes 7864320 | tf_op jit(solution)/shard_map/reduce_scatter | solution.py:74
  7.3 36.2 %copy-start.47 = (pred[192]{0:T(512)(128)(4,1)}, pred[192]{0:T(512)(128)(4,1)S(1)}, u32[]{:S(2)}) copy-start(pred[192]{0:T(512)(128)(4,1)S(1)} %get-tuple-element.690) | copy-start | bytes 580
  7.3 36.2 %copy-start.50 = (pred[192]{0:T(512)(128)(4,1)}, pred[192]{0:T(512)(128)(4,1)S(1)}, u32[]{:S(2)}) copy-start(pred[192]{0:T(512)(128)(4,1)S(1)} %get-tuple-element.689) | copy-start | bytes 580
  7.3 36.7 %copy-start.66 = (s32[1,4]{1,0:T(1,128)S(1)}, s32[1,4]{1,0:T(1,128)}, u32[]{:S(2)}) copy-start(s32[1,4]{1,0:T(1,128)} %param.18) | copy-start | bytes 52
  7.3 37.5 %copy-start.61 = (f32[2,192]{1,0:T(2,128)S(1)}, f32[2,192]{1,0:T(2,128)}, u32[]{:S(2)}) copy-start(f32[2,192]{1,0:T(2,128)} %param.21) | copy-start | bytes 4612
  22.5 20.9 %copy-start.45 = (f32[2048]{0:T(1024)}, f32[2048]{0:T(1024)S(1)}, u32[]{:S(2)}) copy-start(f32[2048]{0:T(1024)S(1)} %get-tuple-element.661) | copy-start | bytes 24580
  22.6 20.9 %copy-start.32 = (f32[2048]{0:T(1024)}, f32[2048]{0:T(1024)S(1)}, u32[]{:S(2)}) copy-start(f32[2048]{0:T(1024)S(1)} %get-tuple-element.687) | copy-start | bytes 24580
  24.1 19.3 %collective-permute-start = (bf16[2048,192]{0,1:T(8,128)(2,1)S(1)}, bf16[2048,192]{0,1:T(8,128)(2,1)}, u32[]{:S(2)}, u32[]{:S(2)}) collective-permute-start(bf16[2048,192]{0,1:T(8,128)(2,1)S(1)} %multiply_convert_fusion.3), channel_id=1, source_target_pairs={{0,1},{1,2},{2,3},{3,0},{4,5},{5,6},{6,7},{7,4},{8,9},{9,10},{10,1... | collective-permute-start | bytes 2359304 | tf_op jit(solution)/shard_map/ppermute | solution.py:58
  24.2 45.7 %collective-permute-start.1 = (bf16[2048,192]{0,1:T(8,128)(2,1)S(1)}, bf16[2048,192]{0,1:T(8,128)(2,1)}, u32[]{:S(2)}, u32[]{:S(2)}) collective-permute-start(bf16[2048,192]{0,1:T(8,128)(2,1)S(1)} %multiply_convert_fusion.3), channel_id=1, source_target_pairs={{0,3},{1,0},{2,1},{3,2},{4,7},{5,4},{6,5},{7,6},{8,11},{9,8},{10,9... | collective-permute-start | bytes 2359304 | tf_op jit(solution)/shard_map/ppermute | solution.py:63
  43.4 39.3 %collective-permute-start.2 = (bf16[2048,192]{0,1:T(8,128)(2,1)}, bf16[2048,192]{0,1:T(8,128)(2,1)}, u32[]{:S(2)}, u32[]{:S(2)}) collective-permute-start(bf16[2048,192]{0,1:T(8,128)(2,1)} %collective-permute-done), channel_id=1, source_target_pairs={{0,1},{1,2},{2,3},{3,0},{4,5},{5,6},{6,7},{7,4},{8,9},{9,10},{10,1... | collective-permute-start | bytes 2359304 | tf_op jit(solution)/shard_map/ppermute | solution.py:58
  200.6 60.0 %copy-start.58 = (f32[192]{0:T(256)S(1)}, f32[192]{0:T(256)}, u32[]{:S(2)}) copy-start(f32[192]{0:T(256)} %param.23) | copy-start | bytes 2308
  200.6 69.4 %copy-start.9 = (bf16[2048,192]{0,1:T(8,128)(2,1)S(1)}, bf16[2048,192]{0,1:T(8,128)(2,1)}, u32[]{:S(2)}) copy-start(bf16[2048,192]{0,1:T(8,128)(2,1)} %param.17) | copy-start | bytes 2359300
  200.6 172.8 %all-gather.3.cloned.1.call-start = ((), (), s32[]{:S(2)}) async-start(), calls=%async_computation.6 | async-start | bytes 3932160 | tf_op jit(solution)/shard_map/all_gather | solution.py:80
  286.9 146.6 %reduce-scatter.9.cloned.1.call-start = ((), (), s32[]{:S(2)}) async-start(), calls=%async_computation.7 | async-start | bytes 3932160 | tf_op jit(solution)/shard_map/reduce_scatter | solution.py:84
  286.9 25.9 %copy-start.34 = (f32[2048]{0:T(1024)}, f32[2048]{0:T(1024)S(1)}, u32[]{:S(2)}) copy-start(f32[2048]{0:T(1024)S(1)} %get-tuple-element.685) | copy-start | bytes 24580
  288.7 24.2 %collective-permute-start.3 = (bf16[2048,192]{0,1:T(8,128)(2,1)S(1)}, bf16[2048,192]{0,1:T(8,128)(2,1)}, u32[]{:S(2)}, u32[]{:S(2)}) collective-permute-start(bf16[2048,192]{0,1:T(8,128)(2,1)S(1)} %multiply_convert_fusion.2), channel_id=1, source_target_pairs={{0,1},{1,2},{2,3},{3,0},{4,5},{5,6},{6,7},{7,4},{8,9},{9,10},{10,1... | collective-permute-start | bytes 2359304 | tf_op jit(solution)/shard_map/ppermute | solution.py:58
  289.4 57.3 %collective-permute-start.4 = (bf16[2048,192]{0,1:T(8,128)(2,1)S(1)}, bf16[2048,192]{0,1:T(8,128)(2,1)}, u32[]{:S(2)}, u32[]{:S(2)}) collective-permute-start(bf16[2048,192]{0,1:T(8,128)(2,1)S(1)} %multiply_convert_fusion.2), channel_id=1, source_target_pairs={{0,3},{1,0},{2,1},{3,2},{4,7},{5,4},{6,5},{7,6},{8,11},{9,8},{10,9... | collective-permute-start | bytes 2359304 | tf_op jit(solution)/shard_map/ppermute | solution.py:63
  312.9 48.0 %collective-permute-start.5 = (bf16[2048,192]{0,1:T(8,128)(2,1)}, bf16[2048,192]{0,1:T(8,128)(2,1)}, u32[]{:S(2)}, u32[]{:S(2)}) collective-permute-start(bf16[2048,192]{0,1:T(8,128)(2,1)} %collective-permute-done.3), channel_id=1, source_target_pairs={{0,1},{1,2},{2,3},{3,0},{4,5},{5,6},{6,7},{7,4},{8,9},{9,10},{10,1... | collective-permute-start | bytes 2359304 | tf_op jit(solution)/shard_map/ppermute | solution.py:58
  392.9 101.4 %reduce-scatter.7.cloned.1.call-start = ((), (), s32[]{:S(2)}) async-start(), calls=%async_computation.5 | async-start | bytes 7864320 | tf_op jit(solution)/shard_map/reduce_scatter | solution.py:74
  400.6 32.8 %copy-start.35 = (f32[2048]{0:T(1024)S(1)}, f32[2048]{0:T(1024)}, u32[]{:S(2)}) copy-start(f32[2048]{0:T(1024)} %copy-done.34) | copy-start | bytes 24580
  400.6 32.8 %copy-start.51 = (pred[192]{0:T(512)(128)(4,1)S(1)}, pred[192]{0:T(512)(128)(4,1)}, u32[]{:S(2)}) copy-start(pred[192]{0:T(512)(128)(4,1)} %copy-done.50) | copy-start | bytes 580
  400.6 32.8 %copy-start.53 = (f32[192]{0:T(256)S(1)}, f32[192]{0:T(256)}, u32[]{:S(2)}) copy-start(f32[192]{0:T(256)} %param.24) | copy-start | bytes 2308
  400.7 93.6 %copy-start.59 = (f32[192]{0:T(256)S(1)}, f32[192]{0:T(256)}, u32[]{:S(2)}) copy-start(f32[192]{0:T(256)} %param.28) | copy-start | bytes 2308
  400.7 105.5 %copy-start.42 = (f32[2048]{0:T(1024)S(1)}, f32[2048]{0:T(1024)}, u32[]{:S(2)}) copy-start(f32[2048]{0:T(1024)} %copy-done.41) | copy-start | bytes 24580
  400.7 105.5 %copy-start.44 = (f32[2048]{0:T(1024)S(1)}, f32[2048]{0:T(1024)}, u32[]{:S(2)}) copy-start(f32[2048]{0:T(1024)} %copy-done.43) | copy-start | bytes 24580
  400.7 105.5 %copy-start.14 = (bf16[2048,192]{0,1:T(8,128)(2,1)S(1)}, bf16[2048,192]{0,1:T(8,128)(2,1)}, u32[]{:S(2)}) copy-start(bf16[2048,192]{0,1:T(8,128)(2,1)} %param.29) | copy-start | bytes 2359300
  400.7 105.5 %copy-start.48 = (pred[192]{0:T(512)(128)(4,1)S(1)}, pred[192]{0:T(512)(128)(4,1)}, u32[]{:S(2)}) copy-start(pred[192]{0:T(512)(128)(4,1)} %copy-done.47) | copy-start | bytes 580
  400.7 142.4 %all-gather.5.cloned.1.call-start = ((), (), s32[]{:S(2)}) async-start(), calls=%async_computation.8 | async-start | bytes 3932160 | tf_op jit(solution)/shard_map/all_gather | solution.py:80
  433.5 72.8 %copy-start.21 = (bf16[2048,192]{0,1:T(8,128)(2,1)S(1)}, bf16[2048,192]{0,1:T(8,128)(2,1)}, u32[]{:S(2)}) copy-start(bf16[2048,192]{0,1:T(8,128)(2,1)} %reduce-scatter.9.cloned.1.call-done) | copy-start | bytes 2359300
  511.1 32.0 %copy-start.28 = (bf16[192,768]{1,0:T(8,128)(2,1)S(1)}, bf16[192,768]{1,0:T(8,128)(2,1)}, u32[]{:S(2)}) copy-start(bf16[192,768]{1,0:T(8,128)(2,1)} %param.22) | copy-start | bytes 884740
  513.4 213.0 %reduce-scatter.11.cloned.1.call-start = ((), (), s32[]{:S(2)}) async-start(), calls=%async_computation.9 | async-start | bytes 3932160 | tf_op jit(solution)/shard_map/reduce_scatter | solution.py:84
  688.3 280.1 %all-reduce.8.cloned.1.call-start = ((), (), s32[]{:S(2)}) async-start(), calls=%async_computation.10 | async-start | bytes 14155776 | tf_op jit(solution)/shard_map/psum | solution.py:331
  704.8 21.6 %copy-start.10 = (bf16[2048,192]{0,1:T(8,128)(2,1)S(1)}, bf16[2048,192]{0,1:T(8,128)(2,1)}, u32[]{:S(2)}) copy-start(bf16[2048,192]{0,1:T(8,128)(2,1)} %param.17) | copy-start | bytes 2359300
  704.8 21.6 %copy-start.15 = (bf16[2048,192]{0,1:T(8,128)(2,1)S(1)}, bf16[2048,192]{0,1:T(8,128)(2,1)}, u32[]{:S(2)}) copy-start(bf16[2048,192]{0,1:T(8,128)(2,1)} %param.29) | copy-start | bytes 2359300
  704.8 21.6 %copy-start.31 = (f32[2048]{0:T(1024)S(1)}, f32[2048]{0:T(1024)}, u32[]{:S(2)}) copy-start(f32[2048]{0:T(1024)} %copy-done.30) | copy-start | bytes 24580
  704.8 21.6 %copy-start.33 = (f32[2048]{0:T(1024)S(1)}, f32[2048]{0:T(1024)}, u32[]{:S(2)}) copy-start(f32[2048]{0:T(1024)} %copy-done.32) | copy-start | bytes 24580
  704.8 21.6 %copy-start.37 = (f32[2048]{0:T(1024)S(1)}, f32[2048]{0:T(1024)}, u32[]{:S(2)}) copy-start(f32[2048]{0:T(1024)} %copy-done.36) | copy-start | bytes 24580
  704.8 21.6 %copy-start.49 = (pred[192]{0:T(512)(128)(4,1)S(1)}, pred[192]{0:T(512)(128)(4,1)}, u32[]{:S(2)}) copy-start(pred[192]{0:T(512)(128)(4,1)} %copy-done.47) | copy-start | bytes 580
  704.8 21.6 %copy-start.52 = (pred[192]{0:T(512)(128)(4,1)S(1)}, pred[192]{0:T(512)(128)(4,1)}, u32[]{:S(2)}) copy-start(pred[192]{0:T(512)(128)(4,1)} %copy-done.50) | copy-start | bytes 580
  704.8 21.6 %copy-start.54 = (f32[192]{0:T(256)S(1)}, f32[192]{0:T(256)}, u32[]{:S(2)}) copy-start(f32[192]{0:T(256)} %param.19) | copy-start | bytes 2308
  705.4 23.3 %copy-start.39 = (f32[2048]{0:T(1024)S(1)}, f32[2048]{0:T(1024)}, u32[]{:S(2)}) copy-start(f32[2048]{0:T(1024)} %get-tuple-element.679) | copy-start | bytes 24580
  705.4 23.3 %copy-start.40 = (f32[2048]{0:T(1024)S(1)}, f32[2048]{0:T(1024)}, u32[]{:S(2)}) copy-start(f32[2048]{0:T(1024)} %get-tuple-element.680) | copy-start | bytes 24580
  705.4 34.9 %copy-start.55 = (f32[192]{0:T(256)S(1)}, f32[192]{0:T(256)}, u32[]{:S(2)}) copy-start(f32[192]{0:T(256)} %get-tuple-element.581) | copy-start | bytes 2308
  705.4 34.9 %copy-start.56 = (f32[192]{0:T(256)S(1)}, f32[192]{0:T(256)}, u32[]{:S(2)}) copy-start(f32[192]{0:T(256)} %get-tuple-element.664) | copy-start | bytes 2308
  705.4 34.9 %copy-start.57 = (f32[768]{0:T(1024)S(1)}, f32[768]{0:T(1024)}, u32[]{:S(2)}) copy-start(f32[768]{0:T(1024)} %get-tuple-element.662) | copy-start | bytes 9220
  705.4 75.3 %copy-start.46 = (f32[2048]{0:T(1024)S(1)}, f32[2048]{0:T(1024)}, u32[]{:S(2)}) copy-start(f32[2048]{0:T(1024)} %copy-done.45) | copy-start | bytes 24580
  705.4 75.3 %copy-start.12 = (f32[2048,192]{0,1:T(8,128)S(1)}, f32[2048,192]{0,1:T(8,128)}, u32[]{:S(2)}) copy-start(f32[2048,192]{0,1:T(8,128)} %copy-done.11) | copy-start | bytes 4718596
  (59 other events, 274.0 us)
Sparse Core Ops, SparseCore 0:
  200.8 59.7 reduce-scatter.4
  287.0 43.9 all-gather.2
  393.0 40.4 reduce-scatter.8
  435.8 58.3 reduce-scatter.6
  513.5 29.5 all-gather.4
  688.4 37.9 reduce-scatter.10
  732.0 236.4 all-reduce.7
